TPU v7x, 128 devices: a whole 4x4x4 slice. The times are simulated.
128 devices in a mesh: band: 4 (over y), tile: 32 (over x, z, core).
Axes of the slice: x: 4, y: 4, z: 4, core: 2. Of those that a mesh axis runs over, the one named last changes fastest.
Arguments:
- winds: float32 [2, 8, 48, 256, 720], P(None, None, 'band', 'tile'), may hold values from -8 to 8
- basis: bfloat16 [24, 48, 2, 256, 720], P(None, 'band', None, 'tile'), may hold values from -48 to 48
- ground: int32 [256, 720], P('tile'), may hold values from 24 to 48
Outputs:
- new_basis: float32 [24, 48, 2, 256, 720], P(None, 'band', None, 'tile')
All inputs are finite; a program needn't handle non-finite values.
Results may differ from a plain program's by a relative error of at most 0.0015.
Values sent between devices are 32-bit elements; how exact they have to be, the bound alone decides.
A program may use at most 128 MiB of HBM per device.

v0:
```python
import functools

import jax
import jax.numpy as jnp
import numpy as np
from jax import lax
from jax.experimental import pallas as pl
from jax.experimental.pallas import tpu as pltpu
from jax.sharding import PartitionSpec as P

ITERS = 4
MESH = pl.DeviceIdType.MESH
HIGH = lax.Precision.HIGHEST
LANES = 128
ROWS = 8


def padded(x, width):
    return jnp.concatenate([x, jnp.zeros((x.shape[0], width - x.shape[1]), x.dtype)], axis=1)


def turned(x, shift, axis):
    shift %= x.shape[axis]
    return x if shift == 0 else pltpu.roll(x, shift, axis)


def gather_kernel(
    bands, tiles, rank, snaps,
    winds, basis, ground, cosine, factor, pick,
    stacked, gram,
    wind, old, cols, send, recv, keep, total, near, far, across,
    wind_sem, old_sem, out_sem, send_sem, recv_sem, near_send, near_recv, far_send, far_recv, across_send, across_recv,
):
    levels = winds.shape[2]
    lat = winds.shape[4]
    width = cols.shape[2]
    near_n, far_n = near.shape[0], far.shape[0]
    quads = snaps // 4
    band = lax.axis_index("band")
    tile = lax.axis_index("tile")
    right = lax.rem(tile + 1, tiles)
    left = lax.rem(tile + tiles - 1, tiles)

    def wind_copy(level):
        return pltpu.make_async_copy(winds.at[:, :, level], wind.at[:, :, level], wind_sem.at[level])

    def old_copy(level):
        return pltpu.make_async_copy(basis.at[:, level], old.at[:, level], old_sem.at[level])

    def out_copy(level):
        return pltpu.make_async_copy(
            cols.at[pl.ds(2 * level, 2)], stacked.at[pl.ds(2 * level, 2)], out_sem.at[level]
        )

    def edge_copy(way, level):
        return pltpu.make_async_remote_copy(
            src_ref=send.at[way, level],
            dst_ref=recv.at[way, level],
            send_sem=send_sem.at[way, level],
            recv_sem=recv_sem.at[way, level],
            device_id=(band, right if way == 0 else left),
            device_id_type=MESH,
        )

    @pl.loop(0, levels)
    def _(level):
        wind_copy(level).start()

    @pl.loop(0, levels)
    def _(level):
        old_copy(level).start()

    near_at = lax.rem(tile, near_n)
    far_at = lax.div(tile, near_n)
    near_peers = [(band, far_at * near_n + lax.rem(near_at + d, near_n)) for d in range(1, near_n)]
    far_peers = [(band, lax.rem(tile + d * near_n, tiles)) for d in range(1, far_n)]
    band_peers = [(lax.rem(band + d, bands), tile) for d in range(1, bands)]
    barrier = pltpu.get_barrier_semaphore()
    greeted = [(band, left), (band, right)] + near_peers + far_peers + band_peers
    for peer in greeted:
        pl.semaphore_signal(barrier, inc=1, device_id=peer, device_id_type=MESH)

    row = lax.broadcasted_iota(jnp.int32, (ROWS, 1), 0)

    def pack(level):
        for field in range(2):
            for quad in range(quads):
                at = [turned(wind[field, 4 * quad + j, level], 2 * j, 0) for j in range(4)]
                slot = pl.ds((field * quads + quad) * ROWS, ROWS)
                send[1, level, slot, :] = jnp.where(
                    row < 2, at[0], jnp.where(row < 4, at[1], jnp.where(row < 6, at[2], at[3]))
                )
                send[0, level, slot, :] = jnp.where(
                    row < 2, at[1], jnp.where(row < 4, at[2], jnp.where(row < 6, at[3], at[0]))
                )

    wind_copy(0).wait()
    pack(0)
    pl.semaphore_wait(barrier, len(greeted))

    @pl.loop(1, levels)
    def _(level):
        wind_copy(level).wait()
        pack(level)
        edge_copy(0, level - 1).start()
        edge_copy(1, level - 1).start()

    keep[...] = padded(ground[...], width)
    total[...] = jnp.zeros_like(total)
    edge_copy(0, levels - 1).start()
    edge_copy(1, levels - 1).start()

    @pl.loop(0, levels)
    def _(level):
        old_copy(level).wait()
        for field in range(2):
            for pair in range(rank // 2):
                two = old[pl.ds(2 * pair, 2), level, field].astype(jnp.float32)
                two = two.reshape(2 * ROWS, lat)
                cols[2 * level + field, pl.ds(2 * ROWS * pair, 2 * ROWS), :] = padded(two, width).astype(jnp.bfloat16)

    def along_lon(x, edge, j):
        after = [row == 2 * j, (row == 2 * j) | (row == 2 * j + 1)]
        edge = turned(jnp.where(after[1], edge[0], edge[1]), -2 * j, 0)
        near_diff = turned(jnp.where(row == 0, edge, x), -1, 0) - turned(jnp.where(row == 7, edge, x), 1, 0)
        far_diff = turned(jnp.where(row < 2, edge, x), -2, 0) - turned(jnp.where(row >= 6, edge, x), 2, 0)
        return 8.0 * near_diff - far_diff

    def along_lat(x):
        near_diff = turned(x, -1, 1) - turned(x, 1, 1)
        far_diff = turned(x, -2, 1) - turned(x, 2, 1)
        return 8.0 * near_diff - far_diff

    def product(level):
        out = None
        for field in range(2):
            m = cols[2 * level + field]
            part = lax.dot_general(m, m, (((1,), (1,)), ((), ())), preferred_element_type=jnp.float32)
            out = part if out is None else out + part
        total[...] += out

    def snapshots(level):
        edge_copy(0, level).wait_recv()
        edge_copy(1, level).wait_recv()
        cos = cosine[...]
        scale = jnp.where(band * levels + level < keep[...], factor[...], 0.0)
        for pair in range(snaps // 2):
            found = [[], []]
            for snap in (2 * pair, 2 * pair + 1):
                quad, j = divmod(snap, 4)
                east, north = (padded(wind[field, snap, level], width) for field in range(2))
                edges = []
                for field in range(2):
                    slot = pl.ds((field * quads + quad) * ROWS, ROWS)
                    edges.append([padded(recv[way, level, slot, :], width) for way in (1, 0)])
                found[0].append((along_lon(north, edges[1], j) - along_lat(east * cos)) * scale)
                found[1].append((along_lon(east, edges[0], j) + along_lat(north * cos)) * scale)
            for field in range(2):
                both = jnp.concatenate(found[field], axis=0).astype(jnp.bfloat16)
                cols[2 * level + field, pl.ds((rank + 2 * pair) * ROWS, 2 * ROWS), :] = both

    snapshots(0)

    @pl.loop(1, levels)
    def _(level):
        product(level - 1)
        snapshots(level)
        out_copy(level - 1).start()

    product(levels - 1)
    out_copy(levels - 1).start()

    side = total.shape[0]
    same = (
        lax.rem(lax.broadcasted_iota(jnp.int32, (ROWS, side), 1), ROWS)
        == lax.broadcasted_iota(jnp.int32, (ROWS, side), 0)
    )
    blocks = jnp.where(same[None], total[...].reshape(side // ROWS, ROWS, side), 0.0).sum(axis=1)
    wide = jnp.dot(blocks, pick[...], precision=HIGH, preferred_element_type=jnp.float32)
    group = lax.div(lax.broadcasted_iota(jnp.int32, (ROWS, LANES), 1), side // ROWS)
    part = wide[0:ROWS]
    for q in range(1, side // ROWS // ROWS):
        part = jnp.where(group == q, wide[q * ROWS : (q + 1) * ROWS], part)

    def summed(part, box, at, peers, sems, sent):
        box[at] = part

        def copy(slot, d, peer):
            return pltpu.make_async_remote_copy(
                src_ref=box.at[slot],
                dst_ref=box.at[slot],
                send_sem=sent.at[d],
                recv_sem=sems.at[slot],
                device_id=peer,
                device_id_type=MESH,
            )

        n = box.shape[0]
        for d, peer in enumerate(peers):
            copy(at, d, peer).start()
        for d, peer in enumerate(peers):
            copy(lax.rem(at + d + 1, n), d, peer).wait_recv()
        out = box[0]
        for slot in range(1, n):
            out = out + box[slot]
        for d, peer in enumerate(peers):
            copy(at, d, peer).wait_send()
        return out

    part = summed(part, near, near_at, near_peers, near_recv, near_send)
    part = summed(part, far, far_at, far_peers, far_recv, far_send)
    part = summed(part, across, band, band_peers, across_recv, across_send)
    gram[...] = part

    @pl.loop(0, levels)
    def _(level):
        edge_copy(0, level).wait_send()
        edge_copy(1, level).wait_send()
        out_copy(level).wait()


def over_rows(x):
    x = x[0:8] + x[8:16] + (x[16:24] + x[24:32])
    for shift in (4, 2, 1):
        x = x + pltpu.roll(x, shift, 0)
    return jnp.concatenate([x] * 4, axis=0)


def orthonormal(wide_ref, rank):
    size = wide_ref.shape[1]
    lane = lax.broadcasted_iota(jnp.int32, (size, LANES), 1)
    columns = [wide_ref[k] for k in range(rank)]
    narrow = jnp.zeros((size, LANES), jnp.float32)
    for k in range(rank):
        column = columns[k]
        square = over_rows(column * column)
        scaled = column * (1.0 / square)
        for j in range(k + 1, rank):
            columns[j] = columns[j] - scaled * over_rows(column * columns[j])
        unit = column * lax.rsqrt(square)
        wide_ref[k] = unit
        narrow = jnp.where(lane == k, unit, narrow)
    return narrow


def project_kernel(
    rank, gram, pick, stacked, new_basis, cols, weights, wide, gram_wide, out, in_sem, out_sem
):
    slabs, side, width = cols.shape
    levels, fields, _, lat = new_basis.shape[1:]
    size = side // ROWS

    def in_copy(slab):
        return pltpu.make_async_copy(stacked.at[slab], cols.at[slab], in_sem.at[slab])

    def out_copy(slab, slot):
        return pltpu.make_async_copy(
            out.at[slot],
            new_basis.at[:, lax.div(slab, fields), lax.rem(slab, fields)],
            out_sem.at[slot],
        )

    @pl.loop(0, slabs)
    def _(slab):
        in_copy(slab).start()

    packed = gram[...]
    for c in range(size):
        column = jnp.concatenate(
            [
                jnp.broadcast_to(packed[:, q * size + c : q * size + c + 1], (ROWS, LANES))
                for q in range(size // ROWS)
            ],
            axis=0,
        )
        gram_wide[c] = column
        if c < rank:
            wide[c] = column

    def times_gram(narrow):
        parts = [None] * 4
        for c in range(size):
            term = gram_wide[c] * narrow[c : c + 1]
            parts[c % 4] = term if parts[c % 4] is None else parts[c % 4] + term
        return (parts[0] + parts[1]) + (parts[2] + parts[3])

    @pl.loop(0, ITERS - 1)
    def _(sweep):
        block = times_gram(orthonormal(wide, rank))
        for k in range(rank):
            wide[k] = jnp.broadcast_to(block[:, k : k + 1], (size, LANES))

    orthonormal(wide, rank)
    frame = orthonormal(wide, rank)

    across = jnp.dot(frame.T, pick[...], precision=HIGH, preferred_element_type=jnp.float32)
    same = (
        lax.rem(lax.broadcasted_iota(jnp.int32, (ROWS, side), 1), ROWS)
        == lax.broadcasted_iota(jnp.int32, (ROWS, side), 0)
    )
    for k in range(rank):
        rows = jnp.where(same, across[k : k + 1], 0.0)
        high = rows.astype(jnp.bfloat16).astype(jnp.float32)
        weights[0, pl.ds(k * ROWS, ROWS), :] = high
        weights[1, pl.ds(k * ROWS, ROWS), :] = rows - high

    slots = out.shape[0]

    @pl.loop(0, slabs)
    def _(slab):
        slot = lax.rem(slab, slots)

        @pl.when(slab >= slots)
        def _():
            out_copy(slab - slots, slot).wait()

        in_copy(slab).wait()
        both = weights[...].reshape(2 * rank * ROWS, side).astype(jnp.bfloat16)
        found = jnp.dot(both, cols[slab], preferred_element_type=jnp.float32)
        found = found[: rank * ROWS] + found[rank * ROWS :]
        out[slot] = found[:, :lat].reshape(rank, ROWS, lat)
        out_copy(slab, slot).start()

    @pl.loop(slabs - slots, slabs)
    def _(slab):
        out_copy(slab, lax.rem(slab, slots)).wait()


def constants(lat, width, size):
    arc = (np.arange(lat, dtype=np.float32) + np.float32(0.5)) * np.float32(np.pi / lat) - np.float32(np.pi / 2)
    cosine = np.zeros((ROWS, width), np.float32)
    factor = np.zeros((ROWS, width), np.float32)
    cosine[:, :lat] = np.cos(arc.astype(np.float64))
    factor[:, :lat] = np.sqrt(cosine[:, :lat].astype(np.float64)) / (12.0 * cosine[:, :lat].astype(np.float64))
    pick = np.zeros((size * ROWS, LANES), np.float32)
    spread = np.zeros((LANES, size * ROWS), np.float32)
    for c in range(size):
        pick[c * ROWS : (c + 1) * ROWS, c::size] = 1.0
        spread[c, c * ROWS : (c + 1) * ROWS] = 1.0
    return cosine, factor, pick, spread


def on_device(bands, tiles, winds, basis, ground):
    snaps, levels, _, lat = winds.shape[1:]
    rank = basis.shape[0]
    size = rank + snaps
    side = size * ROWS
    width = -(-lat // LANES) * LANES
    near_n, far_n = 8, tiles // 8
    cosine, factor, pick, spread = constants(lat, width, size)
    whole = pl.BlockSpec(memory_space=pltpu.VMEM)
    anywhere = pl.BlockSpec(memory_space=pl.ANY)
    edge = (2, levels, 2 * snaps // 4 * ROWS, lat)
    stacked, gram = pl.pallas_call(
        functools.partial(gather_kernel, bands, tiles, rank, snaps),
        out_shape=(
            jax.ShapeDtypeStruct((2 * levels, side, width), jnp.bfloat16),
            jax.ShapeDtypeStruct((ROWS, LANES), jnp.float32),
        ),
        in_specs=[anywhere, anywhere, whole, whole, whole, whole],
        out_specs=(anywhere, whole),
        scratch_shapes=[
            pltpu.VMEM(winds.shape, jnp.float32),
            pltpu.VMEM(basis.shape, jnp.bfloat16),
            pltpu.VMEM((2 * levels, side, width), jnp.bfloat16),
            pltpu.VMEM(edge, jnp.float32),
            pltpu.VMEM(edge, jnp.float32),
            pltpu.VMEM((ROWS, width), jnp.int32),
            pltpu.VMEM((side, side), jnp.float32),
            pltpu.VMEM((near_n, ROWS, LANES), jnp.float32),
            pltpu.VMEM((far_n, ROWS, LANES), jnp.float32),
            pltpu.VMEM((bands, ROWS, LANES), jnp.float32),
            pltpu.SemaphoreType.DMA((levels,)),
            pltpu.SemaphoreType.DMA((levels,)),
            pltpu.SemaphoreType.DMA((levels,)),
            pltpu.SemaphoreType.DMA((2, levels)),
            pltpu.SemaphoreType.DMA((2, levels)),
            pltpu.SemaphoreType.DMA((near_n,)),
            pltpu.SemaphoreType.DMA((near_n,)),
            pltpu.SemaphoreType.DMA((far_n,)),
            pltpu.SemaphoreType.DMA((far_n,)),
            pltpu.SemaphoreType.DMA((bands,)),
            pltpu.SemaphoreType.DMA((bands,)),
        ],
        compiler_params=pltpu.CompilerParams(collective_id=0, has_side_effects=True),
        name="gather",
    )(winds, basis, ground, jnp.asarray(cosine), jnp.asarray(factor), jnp.asarray(pick))
    return pl.pallas_call(
        functools.partial(project_kernel, rank),
        out_shape=jax.ShapeDtypeStruct(basis.shape, jnp.float32),
        in_specs=[whole, whole, anywhere],
        out_specs=anywhere,
        scratch_shapes=[
            pltpu.VMEM((2 * levels, side, width), jnp.bfloat16),
            pltpu.VMEM((2, rank * ROWS, side), jnp.float32),
            pltpu.VMEM((rank, size, LANES), jnp.float32),
            pltpu.VMEM((size, size, LANES), jnp.float32),
            pltpu.VMEM((4, rank, ROWS, lat), jnp.float32),
            pltpu.SemaphoreType.DMA((2 * levels,)),
            pltpu.SemaphoreType.DMA((4,)),
        ],
        name="project",
    )(gram, jnp.asarray(spread[:size]), stacked)


def solution(mesh):
    return jax.shard_map(
        functools.partial(on_device, mesh.shape["band"], mesh.shape["tile"]),
        mesh=mesh,
        in_specs=(
            P(None, None, "band", "tile", None),
            P(None, "band", None, "tile", None),
            P("tile", None),
        ),
        out_specs=P(None, "band", None, "tile", None),
        check_vma=False,
    )
```

profile of v0, /device:TPU:0, one launch (start us, length us, event | category | flops | bytes accessed | tf_op | source)
XLA Modules:
  0.0 52.5 jit_solution(1568786131095931681)
XLA Ops:
  0.0 37.0 %gather.1 = (bf16[24,256,768]{2,1,0:T(8,128)(2,1)}, f32[8,128]{1,0:T(8,128)}) custom-call(f32[2,8,12,8,720]{4,3,2,1,0:T(8,128)} %winds.1, bf16[24,12,2,8,720]{4,3,2,1,0:T(8,128)(2,1)} %basis.1, s32[8,720]{1,0:T(8,128)} %ground.1, f32[8,768]{1,0:T(8,128)} %constant.8.clone.cosine, f32[8,768]{1,0:T(8,128)} %constant.9.clone.factor, f32[256,128]{1,0:T(8,128)} %constant.10.clone.pick), custom_call_target="tpu_custom_call" | custom-call | tf_op jit(solution)/shard_map/gather/pallas_call | solution.py:354
  37.0 15.5 %project.1 = f32[24,12,2,8,720]{4,3,2,1,0:T(8,128)} custom-call(f32[8,128]{1,0:T(8,128)} %get-tuple-element.7.gram, f32[32,256]{1,0:T(8,128)} %constant.11.clone.pick, bf16[24,256,768]{2,1,0:T(8,128)(2,1)} %get-tuple-element.8.stacked), custom_call_target="tpu_custom_call" | custom-call | tf_op jit(solution)/shard_map/project/pallas_call | solution.py:388
where the time goes:
time: 52.7 us; the launch traced here: 52.5 us
  Pallas kernels  52.5 us (100%)
    pallas_call x1, Pallas kernels, on_device(): pl.pallas_call(functools.partial(gather_kernel, bands, tiles, rank, snaps...  37 us
    pallas_call x1, Pallas kernels, on_device(): pl.pallas_call(functools.partial(project_kernel, rank), out_shape=jax.Sha...  15.5 us

commit v1 on v0

--- a/solution.py
+++ b/solution.py
@@ -13,6 +13,9 @@
 HIGH = lax.Precision.HIGHEST
 LANES = 128
 ROWS = 8
+SLOTS = 4
+GATHER_VMEM = 36 << 20
+PROJECT_VMEM = 24 << 20
 
 
 def padded(x, width):
@@ -24,12 +27,21 @@
     return x if shift == 0 else pltpu.roll(x, shift, axis)
 
 
+def in_pieces(x, count):
+    pieces = []
+    for _ in range(count):
+        piece = x.astype(jnp.bfloat16).astype(jnp.float32)
+        pieces.append(piece)
+        x = x - piece
+    return pieces
+
+
 def gather_kernel(
     bands, tiles, rank, snaps,
-    winds, basis, ground, cosine, factor, pick,
-    stacked, gram,
-    wind, old, cols, send, recv, keep, total, near, far, across,
-    wind_sem, old_sem, out_sem, send_sem, recv_sem, near_send, near_recv, far_send, far_recv, across_send, across_recv,
+    winds, basis, ground_in, cosine_in, factor_in,
+    cols, gram,
+    wind, old, send, recv, ground, cosine, factor, keep, total, near, far, across,
+    small_sem, wind_sem, old_sem, send_sem, recv_sem, near_send, near_recv, far_send, far_recv, across_send, across_recv,
 ):
     levels = winds.shape[2]
     lat = winds.shape[4]
@@ -47,11 +59,6 @@
     def old_copy(level):
         return pltpu.make_async_copy(basis.at[:, level], old.at[:, level], old_sem.at[level])
 
-    def out_copy(level):
-        return pltpu.make_async_copy(
-            cols.at[pl.ds(2 * level, 2)], stacked.at[pl.ds(2 * level, 2)], out_sem.at[level]
-        )
-
     def edge_copy(way, level):
         return pltpu.make_async_remote_copy(
             src_ref=send.at[way, level],
@@ -62,14 +69,6 @@
             device_id_type=MESH,
         )
 
-    @pl.loop(0, levels)
-    def _(level):
-        wind_copy(level).start()
-
-    @pl.loop(0, levels)
-    def _(level):
-        old_copy(level).start()
-
     near_at = lax.rem(tile, near_n)
     far_at = lax.div(tile, near_n)
     near_peers = [(band, far_at * near_n + lax.rem(near_at + d, near_n)) for d in range(1, near_n)]
@@ -80,19 +79,63 @@
     for peer in greeted:
         pl.semaphore_signal(barrier, inc=1, device_id=peer, device_id_type=MESH)
 
+    @pl.loop(0, levels)
+    def _(level):
+        wind_copy(level).start()
+
+    small = [
+        pltpu.make_async_copy(source, held, small_sem.at[i])
+        for i, (source, held) in enumerate(((ground_in, ground), (cosine_in, cosine), (factor_in, factor)))
+    ]
+    for copy in small:
+        copy.start()
+
+    @pl.loop(0, levels)
+    def _(level):
+        old_copy(level).start()
+
     row = lax.broadcasted_iota(jnp.int32, (ROWS, 1), 0)
 
+    lane = lax.broadcasted_iota(jnp.int32, (1, LANES), 1)
+    full = lat // LANES
+    rest = lat - full * LANES
+    groups = 2 * quads
+
     def pack(level):
+        tails = [[], []]
         for field in range(2):
             for quad in range(quads):
                 at = [turned(wind[field, 4 * quad + j, level], 2 * j, 0) for j in range(4)]
-                slot = pl.ds((field * quads + quad) * ROWS, ROWS)
-                send[1, level, slot, :] = jnp.where(
-                    row < 2, at[0], jnp.where(row < 4, at[1], jnp.where(row < 6, at[2], at[3]))
-                )
-                send[0, level, slot, :] = jnp.where(
-                    row < 2, at[1], jnp.where(row < 4, at[2], jnp.where(row < 6, at[3], at[0]))
-                )
+                at = [[x[:, t * LANES : min((t + 1) * LANES, lat)] for t in range(full + 1)] for x in at]
+                for way, order in ((1, (0, 1, 2, 3)), (0, (1, 2, 3, 0))):
+                    for t in range(full + 1):
+                        a, b, c, d = (at[j][t] for j in order)
+                        tile_of = jnp.where(row < 2, a, jnp.where(row < 4, b, jnp.where(row < 6, c, d)))
+                        if t < full:
+                            slot = ((field * quads + quad) * full + t) * ROWS
+                            send[way, level, pl.ds(slot, ROWS), :] = tile_of
+                        else:
+                            tails[way].append(padded(tile_of, LANES))
+        for way in range(2):
+            first, second, third, split = tails[way]
+            first = jnp.where(lane < rest, first, pltpu.roll(split, rest, 1))
+            second = jnp.where(lane < rest, second, pltpu.roll(split, 2 * rest - LANES, 1))
+            for t, x in enumerate((first, second, third)):
+                send[way, level, pl.ds((groups * full + t) * ROWS, ROWS), :] = x
+
+    def edges_of(way, level):
+        found = [
+            [recv[way, level, pl.ds((group * full + t) * ROWS, ROWS), :] for t in range(full)] for group in range(groups)
+        ]
+        first, second, third = (
+            recv[way, level, pl.ds((groups * full + t) * ROWS, ROWS), :] for t in range(groups - 1)
+        )
+        split = jnp.where(
+            lane < LANES - rest,
+            pltpu.roll(first, LANES - rest, 1),
+            pltpu.roll(second, 2 * LANES - 2 * rest, 1),
+        )
+        return [jnp.concatenate(x + [tail], axis=1) for x, tail in zip(found, (first, second, third, split))]
 
     wind_copy(0).wait()
     pack(0)
@@ -105,6 +148,8 @@
         edge_copy(0, level - 1).start()
         edge_copy(1, level - 1).start()
 
+    for copy in small:
+        copy.wait()
     keep[...] = padded(ground[...], width)
     total[...] = jnp.zeros_like(total)
     edge_copy(0, levels - 1).start()
@@ -144,15 +189,13 @@
         edge_copy(1, level).wait_recv()
         cos = cosine[...]
         scale = jnp.where(band * levels + level < keep[...], factor[...], 0.0)
+        arrived = [edges_of(way, level) for way in range(2)]
         for pair in range(snaps // 2):
             found = [[], []]
             for snap in (2 * pair, 2 * pair + 1):
                 quad, j = divmod(snap, 4)
                 east, north = (padded(wind[field, snap, level], width) for field in range(2))
-                edges = []
-                for field in range(2):
-                    slot = pl.ds((field * quads + quad) * ROWS, ROWS)
-                    edges.append([padded(recv[way, level, slot, :], width) for way in (1, 0)])
+                edges = [[arrived[way][field * quads + quad] for way in (1, 0)] for field in range(2)]
                 found[0].append((along_lon(north, edges[1], j) - along_lat(east * cos)) * scale)
                 found[1].append((along_lon(east, edges[0], j) + along_lat(north * cos)) * scale)
             for field in range(2):
@@ -165,10 +208,8 @@
     def _(level):
         product(level - 1)
         snapshots(level)
-        out_copy(level - 1).start()
 
     product(levels - 1)
-    out_copy(levels - 1).start()
 
     side = total.shape[0]
     same = (
@@ -176,8 +217,18 @@
         == lax.broadcasted_iota(jnp.int32, (ROWS, side), 0)
     )
     blocks = jnp.where(same[None], total[...].reshape(side // ROWS, ROWS, side), 0.0).sum(axis=1)
-    wide = jnp.dot(blocks, pick[...], precision=HIGH, preferred_element_type=jnp.float32)
-    group = lax.div(lax.broadcasted_iota(jnp.int32, (ROWS, LANES), 1), side // ROWS)
+    size = side // ROWS
+    pick = lax.div(lax.broadcasted_iota(jnp.int32, (side, LANES), 0), ROWS) == lax.rem(
+        lax.broadcasted_iota(jnp.int32, (side, LANES), 1), size
+    )
+    pieces = in_pieces(blocks, 3)
+    wide = jnp.dot(
+        jnp.concatenate(pieces, axis=0).astype(jnp.bfloat16),
+        pick.astype(jnp.float32).astype(jnp.bfloat16),
+        preferred_element_type=jnp.float32,
+    )
+    wide = wide[:size] + (wide[size : 2 * size] + wide[2 * size :])
+    group = lax.div(lax.broadcasted_iota(jnp.int32, (ROWS, LANES), 1), size)
     part = wide[0:ROWS]
     for q in range(1, side // ROWS // ROWS):
         part = jnp.where(group == q, wide[q * ROWS : (q + 1) * ROWS], part)
@@ -216,7 +267,6 @@
     def _(level):
         edge_copy(0, level).wait_send()
         edge_copy(1, level).wait_send()
-        out_copy(level).wait()
 
 
 def over_rows(x):
@@ -244,25 +294,14 @@
 
 
 def project_kernel(
-    rank, gram, pick, stacked, new_basis, cols, weights, wide, gram_wide, out, in_sem, out_sem
+    rank, gram, cols, new_basis, weights, wide, gram_wide, out, out_sem
 ):
     slabs, side, width = cols.shape
     levels, fields, _, lat = new_basis.shape[1:]
     size = side // ROWS
 
-    def in_copy(slab):
-        return pltpu.make_async_copy(stacked.at[slab], cols.at[slab], in_sem.at[slab])
-
-    def out_copy(slab, slot):
-        return pltpu.make_async_copy(
-            out.at[slot],
-            new_basis.at[:, lax.div(slab, fields), lax.rem(slab, fields)],
-            out_sem.at[slot],
-        )
-
-    @pl.loop(0, slabs)
-    def _(slab):
-        in_copy(slab).start()
+    def out_copy(level, slot):
+        return pltpu.make_async_copy(out.at[slot], new_basis.at[:, level], out_sem.at[slot])
 
     packed = gram[...]
     for c in range(size):
@@ -293,51 +332,55 @@
     orthonormal(wide, rank)
     frame = orthonormal(wide, rank)
 
-    across = jnp.dot(frame.T, pick[...], precision=HIGH, preferred_element_type=jnp.float32)
+    spread = lax.broadcasted_iota(jnp.int32, (size, side), 0) == lax.div(
+        lax.broadcasted_iota(jnp.int32, (size, side), 1), ROWS
+    )
+    pieces = [piece.T[:rank] for piece in in_pieces(frame, 2)]
+    across = jnp.dot(
+        jnp.concatenate(pieces, axis=0).astype(jnp.bfloat16),
+        spread.astype(jnp.float32).astype(jnp.bfloat16),
+        preferred_element_type=jnp.float32,
+    )
     same = (
         lax.rem(lax.broadcasted_iota(jnp.int32, (ROWS, side), 1), ROWS)
         == lax.broadcasted_iota(jnp.int32, (ROWS, side), 0)
     )
     for k in range(rank):
-        rows = jnp.where(same, across[k : k + 1], 0.0)
-        high = rows.astype(jnp.bfloat16).astype(jnp.float32)
-        weights[0, pl.ds(k * ROWS, ROWS), :] = high
-        weights[1, pl.ds(k * ROWS, ROWS), :] = rows - high
+        rows = [jnp.where(same, across[2 * k + i : 2 * k + i + 1], 0.0) for i in range(2)]
+        weights[pl.ds(2 * k * ROWS, 2 * ROWS), :] = jnp.concatenate(rows, axis=0).astype(jnp.bfloat16)
 
     slots = out.shape[0]
 
-    @pl.loop(0, slabs)
-    def _(slab):
-        slot = lax.rem(slab, slots)
-
-        @pl.when(slab >= slots)
+    @pl.loop(0, levels)
+    def _(level):
+        slot = lax.rem(level, slots)
+
+        @pl.when(level >= slots)
         def _():
-            out_copy(slab - slots, slot).wait()
-
-        in_copy(slab).wait()
-        both = weights[...].reshape(2 * rank * ROWS, side).astype(jnp.bfloat16)
-        found = jnp.dot(both, cols[slab], preferred_element_type=jnp.float32)
-        found = found[: rank * ROWS] + found[rank * ROWS :]
-        out[slot] = found[:, :lat].reshape(rank, ROWS, lat)
-        out_copy(slab, slot).start()
-
-    @pl.loop(slabs - slots, slabs)
-    def _(slab):
-        out_copy(slab, lax.rem(slab, slots)).wait()
-
-
-def constants(lat, width, size):
+            out_copy(level - slots, slot).wait()
+
+        for field in range(fields):
+            found = jnp.dot(weights[...], cols[fields * level + field], preferred_element_type=jnp.float32)
+            found = found[: rank * ROWS] + found[rank * ROWS :]
+            out[slot, :, field] = found[:, :lat].reshape(rank, ROWS, lat)
+        out_copy(level, slot).start()
+
+    @pl.loop(levels - slots, levels)
+    def _(level):
+        out_copy(level, lax.rem(level, slots)).wait()
+
+
+def in_hbm(x):
+    return pltpu.with_memory_space_constraint(x, pltpu.HBM)
+
+
+def constants(lat, width):
     arc = (np.arange(lat, dtype=np.float32) + np.float32(0.5)) * np.float32(np.pi / lat) - np.float32(np.pi / 2)
     cosine = np.zeros((ROWS, width), np.float32)
     factor = np.zeros((ROWS, width), np.float32)
     cosine[:, :lat] = np.cos(arc.astype(np.float64))
     factor[:, :lat] = np.sqrt(cosine[:, :lat].astype(np.float64)) / (12.0 * cosine[:, :lat].astype(np.float64))
-    pick = np.zeros((size * ROWS, LANES), np.float32)
-    spread = np.zeros((LANES, size * ROWS), np.float32)
-    for c in range(size):
-        pick[c * ROWS : (c + 1) * ROWS, c::size] = 1.0
-        spread[c, c * ROWS : (c + 1) * ROWS] = 1.0
-    return cosine, factor, pick, spread
+    return cosine, factor
 
 
 def on_device(bands, tiles, winds, basis, ground):
@@ -347,30 +390,32 @@
     side = size * ROWS
     width = -(-lat // LANES) * LANES
     near_n, far_n = 8, tiles // 8
-    cosine, factor, pick, spread = constants(lat, width, size)
+    cosine, factor = constants(lat, width)
     whole = pl.BlockSpec(memory_space=pltpu.VMEM)
-    anywhere = pl.BlockSpec(memory_space=pl.ANY)
-    edge = (2, levels, 2 * snaps // 4 * ROWS, lat)
+    anywhere = pl.BlockSpec(memory_space=pltpu.HBM)
+    edge = (2, levels, (snaps // 2 * (lat // LANES) + snaps // 2 - 1) * ROWS, LANES)
     stacked, gram = pl.pallas_call(
         functools.partial(gather_kernel, bands, tiles, rank, snaps),
         out_shape=(
             jax.ShapeDtypeStruct((2 * levels, side, width), jnp.bfloat16),
             jax.ShapeDtypeStruct((ROWS, LANES), jnp.float32),
         ),
-        in_specs=[anywhere, anywhere, whole, whole, whole, whole],
-        out_specs=(anywhere, whole),
+        in_specs=[anywhere] * 5,
+        out_specs=(whole, whole),
         scratch_shapes=[
             pltpu.VMEM(winds.shape, jnp.float32),
             pltpu.VMEM(basis.shape, jnp.bfloat16),
-            pltpu.VMEM((2 * levels, side, width), jnp.bfloat16),
             pltpu.VMEM(edge, jnp.float32),
             pltpu.VMEM(edge, jnp.float32),
+            pltpu.VMEM(ground.shape, jnp.int32),
+            pltpu.VMEM((ROWS, width), jnp.float32),
+            pltpu.VMEM((ROWS, width), jnp.float32),
             pltpu.VMEM((ROWS, width), jnp.int32),
             pltpu.VMEM((side, side), jnp.float32),
             pltpu.VMEM((near_n, ROWS, LANES), jnp.float32),
             pltpu.VMEM((far_n, ROWS, LANES), jnp.float32),
             pltpu.VMEM((bands, ROWS, LANES), jnp.float32),
-            pltpu.SemaphoreType.DMA((levels,)),
+            pltpu.SemaphoreType.DMA((3,)),
             pltpu.SemaphoreType.DMA((levels,)),
             pltpu.SemaphoreType.DMA((levels,)),
             pltpu.SemaphoreType.DMA((2, levels)),
@@ -382,25 +427,24 @@
             pltpu.SemaphoreType.DMA((bands,)),
             pltpu.SemaphoreType.DMA((bands,)),
         ],
-        compiler_params=pltpu.CompilerParams(collective_id=0, has_side_effects=True),
+        compiler_params=pltpu.CompilerParams(collective_id=0, has_side_effects=True, vmem_limit_bytes=GATHER_VMEM),
         name="gather",
-    )(winds, basis, ground, jnp.asarray(cosine), jnp.asarray(factor), jnp.asarray(pick))
+    )(*(in_hbm(x) for x in (winds, basis, ground, jnp.asarray(cosine), jnp.asarray(factor))))
     return pl.pallas_call(
         functools.partial(project_kernel, rank),
         out_shape=jax.ShapeDtypeStruct(basis.shape, jnp.float32),
-        in_specs=[whole, whole, anywhere],
+        in_specs=[whole, whole],
         out_specs=anywhere,
         scratch_shapes=[
-            pltpu.VMEM((2 * levels, side, width), jnp.bfloat16),
-            pltpu.VMEM((2, rank * ROWS, side), jnp.float32),
+            pltpu.VMEM((2 * rank * ROWS, side), jnp.bfloat16),
             pltpu.VMEM((rank, size, LANES), jnp.float32),
             pltpu.VMEM((size, size, LANES), jnp.float32),
-            pltpu.VMEM((4, rank, ROWS, lat), jnp.float32),
-            pltpu.SemaphoreType.DMA((2 * levels,)),
-            pltpu.SemaphoreType.DMA((4,)),
+            pltpu.VMEM((SLOTS, rank, 2, ROWS, lat), jnp.float32),
+            pltpu.SemaphoreType.DMA((SLOTS,)),
         ],
+        compiler_params=pltpu.CompilerParams(vmem_limit_bytes=PROJECT_VMEM),
         name="project",
-    )(gram, jnp.asarray(spread[:size]), stacked)
+    )(gram, stacked)
 
 
 def solution(mesh):

time: 52.7 us -> 47.4 us (0.90)
  Pallas kernels: 52.5 us -> 47.3 us
    pallas_call x1, Pallas kernels: 15.5 us -> 12.6 us  [on_device(): pl.pallas_call(functools.partial(project_kernel, rank), out_shape=jax.Sha...]
    pallas_call x1, Pallas kernels: 37 us -> 34.8 us  [on_device(): pl.pallas_call(functools.partial(gather_kernel, bands, tiles, rank, snaps...]
where the time goes in v1:
time: 47.4 us; the launch traced here: 47.3 us
  Pallas kernels  47.3 us (100%)
    pallas_call x1, Pallas kernels, on_device(): pl.pallas_call(functools.partial(gather_kernel, bands, tiles, rank, snaps...  34.8 us
    pallas_call x1, Pallas kernels, on_device(): pl.pallas_call(functools.partial(project_kernel, rank), out_shape=jax.Sha...  12.6 us

profile of v1, /device:TPU:0, one launch (start us, length us, event | category | flops | bytes accessed | tf_op | source)
XLA Modules:
  0.0 47.3 jit_solution(14432860754872301242)
XLA Ops:
  0.0 34.8 %gather.1 = (bf16[24,256,768]{2,1,0:T(8,128)(2,1)S(1)}, f32[8,128]{1,0:T(8,128)S(1)}) custom-call(f32[2,8,12,8,720]{4,3,2,1,0:T(8,128)} %winds.1, bf16[24,12,2,8,720]{4,3,2,1,0:T(8,128)(2,1)} %basis.1, s32[8,720]{1,0:T(8,128)} %ground_in.1, f32[8,768]{1,0:T(8,128)} %constant.4.clone.cosine_in, f32[8,768]{1,0:T(8,128)} %constant.5.clone.factor_in), custom_call_target="tpu_custom_call" | custom-call | tf_op jit(solution)/shard_map/gather/pallas_call | solution.py:397
  34.8 12.6 %project.1 = f32[24,12,2,8,720]{4,3,2,1,0:T(8,128)} custom-call(f32[8,128]{1,0:T(8,128)S(1)} %get-tuple-element.7.gram, bf16[24,256,768]{2,1,0:T(8,128)(2,1)S(1)} %get-tuple-element.8.cols), custom_call_target="tpu_custom_call" | custom-call | tf_op jit(solution)/shard_map/project/pallas_call | solution.py:433

commit v2 on v1

--- a/solution.py
+++ b/solution.py
@@ -10,7 +10,6 @@
 
 ITERS = 4
 MESH = pl.DeviceIdType.MESH
-HIGH = lax.Precision.HIGHEST
 LANES = 128
 ROWS = 8
 SLOTS = 4
@@ -69,6 +68,7 @@
             device_id_type=MESH,
         )
 
+    wind_copy(0).start()
     near_at = lax.rem(tile, near_n)
     far_at = lax.div(tile, near_n)
     near_peers = [(band, far_at * near_n + lax.rem(near_at + d, near_n)) for d in range(1, near_n)]
@@ -79,7 +79,7 @@
     for peer in greeted:
         pl.semaphore_signal(barrier, inc=1, device_id=peer, device_id_type=MESH)
 
-    @pl.loop(0, levels)
+    @pl.loop(1, levels)
     def _(level):
         wind_copy(level).start()
 
@@ -89,10 +89,6 @@
     ]
     for copy in small:
         copy.start()
-
-    @pl.loop(0, levels)
-    def _(level):
-        old_copy(level).start()
 
     row = lax.broadcasted_iota(jnp.int32, (ROWS, 1), 0)
 
@@ -147,6 +143,9 @@
         pack(level)
         edge_copy(0, level - 1).start()
         edge_copy(1, level - 1).start()
+        old_copy(level - 1).start()
+
+    old_copy(levels - 1).start()
 
     for copy in small:
         copy.wait()
@@ -276,25 +275,28 @@
     return jnp.concatenate([x] * 4, axis=0)
 
 
-def orthonormal(wide_ref, rank):
-    size = wide_ref.shape[1]
+def orthonormal(block, rank):
+    size = block.shape[0]
     lane = lax.broadcasted_iota(jnp.int32, (size, LANES), 1)
-    columns = [wide_ref[k] for k in range(rank)]
-    narrow = jnp.zeros((size, LANES), jnp.float32)
-    for k in range(rank):
-        column = columns[k]
-        square = over_rows(column * column)
-        scaled = column * (1.0 / square)
-        for j in range(k + 1, rank):
-            columns[j] = columns[j] - scaled * over_rows(column * columns[j])
-        unit = column * lax.rsqrt(square)
-        wide_ref[k] = unit
-        narrow = jnp.where(lane == k, unit, narrow)
-    return narrow
+    frame = jnp.zeros((size, LANES), jnp.float32)
+    for first in range(0, rank, ROWS):
+        ids = range(first, min(first + ROWS, rank))
+        columns = {k: jnp.broadcast_to(block[:, k : k + 1], (size, LANES)) for k in ids}
+        for k in ids:
+            column = columns[k]
+            square = over_rows(column * column)
+            scaled = column * (1.0 / square)
+            for j in ids:
+                if j > k:
+                    columns[j] = columns[j] - scaled * over_rows(column * columns[j])
+            if first + ROWS < rank:
+                block = block - scaled * over_rows(column * block)
+            frame = jnp.where(lane == k, column * lax.rsqrt(square), frame)
+    return frame
 
 
 def project_kernel(
-    rank, gram, cols, new_basis, weights, wide, gram_wide, out, out_sem
+    rank, gram, cols, new_basis, weights, gram_wide, out, out_sem
 ):
     slabs, side, width = cols.shape
     levels, fields, _, lat = new_basis.shape[1:]
@@ -304,33 +306,20 @@
         return pltpu.make_async_copy(out.at[slot], new_basis.at[:, level], out_sem.at[slot])
 
     packed = gram[...]
+    block = jnp.concatenate([turned(packed, -q * size, 1) for q in range(size // ROWS)], axis=0)
     for c in range(size):
-        column = jnp.concatenate(
-            [
-                jnp.broadcast_to(packed[:, q * size + c : q * size + c + 1], (ROWS, LANES))
-                for q in range(size // ROWS)
-            ],
-            axis=0,
-        )
-        gram_wide[c] = column
-        if c < rank:
-            wide[c] = column
-
-    def times_gram(narrow):
+        gram_wide[c] = jnp.broadcast_to(block[:, c : c + 1], (size, LANES))
+
+    def times_gram(frame):
         parts = [None] * 4
         for c in range(size):
-            term = gram_wide[c] * narrow[c : c + 1]
+            term = gram_wide[c] * frame[c : c + 1]
             parts[c % 4] = term if parts[c % 4] is None else parts[c % 4] + term
         return (parts[0] + parts[1]) + (parts[2] + parts[3])
 
-    @pl.loop(0, ITERS - 1)
-    def _(sweep):
-        block = times_gram(orthonormal(wide, rank))
-        for k in range(rank):
-            wide[k] = jnp.broadcast_to(block[:, k : k + 1], (size, LANES))
-
-    orthonormal(wide, rank)
-    frame = orthonormal(wide, rank)
+    for sweep in range(ITERS - 1):
+        block = times_gram(orthonormal(block, rank))
+    frame = orthonormal(orthonormal(block, rank), rank)
 
     spread = lax.broadcasted_iota(jnp.int32, (size, side), 0) == lax.div(
         lax.broadcasted_iota(jnp.int32, (size, side), 1), ROWS
@@ -437,7 +426,6 @@
         out_specs=anywhere,
         scratch_shapes=[
             pltpu.VMEM((2 * rank * ROWS, side), jnp.bfloat16),
-            pltpu.VMEM((rank, size, LANES), jnp.float32),
             pltpu.VMEM((size, size, LANES), jnp.float32),
             pltpu.VMEM((SLOTS, rank, 2, ROWS, lat), jnp.float32),
             pltpu.SemaphoreType.DMA((SLOTS,)),

time: 47.4 us -> 45.8 us (0.966)
  Pallas kernels: 47.3 us -> 45.7 us
    pallas_call x1, Pallas kernels: 12.6 us -> 10.9 us  [on_device(): pl.pallas_call(functools.partial(project_kernel, rank), out_shape=jax.Sha...]
where the time goes in v2:
time: 45.8 us; the launch traced here: 45.7 us
  Pallas kernels  45.7 us (100%)
    pallas_call x1, Pallas kernels, on_device(): pl.pallas_call(functools.partial(gather_kernel, bands, tiles, rank, snaps...  34.8 us
    pallas_call x1, Pallas kernels, on_device(): pl.pallas_call(functools.partial(project_kernel, rank), out_shape=jax.Sha...  10.9 us

profile of v2, /device:TPU:0, one launch (start us, length us, event | category | flops | bytes accessed | tf_op | source)
XLA Modules:
  0.0 45.7 jit_solution(16248098789863747886)
XLA Ops:
  0.0 34.8 %gather.1 = (bf16[24,256,768]{2,1,0:T(8,128)(2,1)S(1)}, f32[8,128]{1,0:T(8,128)S(1)}) custom-call(f32[2,8,12,8,720]{4,3,2,1,0:T(8,128)} %winds.1, bf16[24,12,2,8,720]{4,3,2,1,0:T(8,128)(2,1)} %basis.1, s32[8,720]{1,0:T(8,128)} %ground_in.1, f32[8,768]{1,0:T(8,128)} %constant.4.clone.cosine_in, f32[8,768]{1,0:T(8,128)} %constant.5.clone.factor_in), custom_call_target="tpu_custom_call" | custom-call | tf_op jit(solution)/shard_map/gather/pallas_call | solution.py:386
  34.8 10.9 %project.1 = f32[24,12,2,8,720]{4,3,2,1,0:T(8,128)} custom-call(f32[8,128]{1,0:T(8,128)S(1)} %get-tuple-element.7.gram, bf16[24,256,768]{2,1,0:T(8,128)(2,1)S(1)} %get-tuple-element.8.cols), custom_call_target="tpu_custom_call" | custom-call | tf_op jit(solution)/shard_map/project/pallas_call | solution.py:422

commit v3 on v2

--- a/solution.py
+++ b/solution.py
@@ -58,12 +58,21 @@
     def old_copy(level):
         return pltpu.make_async_copy(basis.at[:, level], old.at[:, level], old_sem.at[level])
 
-    def edge_copy(way, level):
+    lane = lax.broadcasted_iota(jnp.int32, (1, LANES), 1)
+    full = lat // LANES
+    rest = lat - full * LANES
+    half_tiles = (2 * full + 2, 2 * full + 1)
+
+    def edge_slot(quad, field, t):
+        return pl.ds((quad * half_tiles[0] + field * full + t) * ROWS, ROWS)
+
+    def edge_copy(way, level, quad):
+        rows = pl.ds(quad * half_tiles[0] * ROWS, half_tiles[quad] * ROWS)
         return pltpu.make_async_remote_copy(
-            src_ref=send.at[way, level],
-            dst_ref=recv.at[way, level],
-            send_sem=send_sem.at[way, level],
-            recv_sem=recv_sem.at[way, level],
+            src_ref=send.at[way, level, rows],
+            dst_ref=recv.at[way, level, rows],
+            send_sem=send_sem.at[way, level, quad],
+            recv_sem=recv_sem.at[way, level, quad],
             device_id=(band, right if way == 0 else left),
             device_id_type=MESH,
         )
@@ -92,15 +101,10 @@
 
     row = lax.broadcasted_iota(jnp.int32, (ROWS, 1), 0)
 
-    lane = lax.broadcasted_iota(jnp.int32, (1, LANES), 1)
-    full = lat // LANES
-    rest = lat - full * LANES
-    groups = 2 * quads
-
     def pack(level):
         tails = [[], []]
-        for field in range(2):
-            for quad in range(quads):
+        for quad in range(quads):
+            for field in range(2):
                 at = [turned(wind[field, 4 * quad + j, level], 2 * j, 0) for j in range(4)]
                 at = [[x[:, t * LANES : min((t + 1) * LANES, lat)] for t in range(full + 1)] for x in at]
                 for way, order in ((1, (0, 1, 2, 3)), (0, (1, 2, 3, 0))):
@@ -108,30 +112,32 @@
                         a, b, c, d = (at[j][t] for j in order)
                         tile_of = jnp.where(row < 2, a, jnp.where(row < 4, b, jnp.where(row < 6, c, d)))
                         if t < full:
-                            slot = ((field * quads + quad) * full + t) * ROWS
-                            send[way, level, pl.ds(slot, ROWS), :] = tile_of
+                            send[way, level, edge_slot(quad, field, t), :] = tile_of
                         else:
                             tails[way].append(padded(tile_of, LANES))
         for way in range(2):
             first, second, third, split = tails[way]
             first = jnp.where(lane < rest, first, pltpu.roll(split, rest, 1))
             second = jnp.where(lane < rest, second, pltpu.roll(split, 2 * rest - LANES, 1))
-            for t, x in enumerate((first, second, third)):
-                send[way, level, pl.ds((groups * full + t) * ROWS, ROWS), :] = x
-
-    def edges_of(way, level):
-        found = [
-            [recv[way, level, pl.ds((group * full + t) * ROWS, ROWS), :] for t in range(full)] for group in range(groups)
-        ]
-        first, second, third = (
-            recv[way, level, pl.ds((groups * full + t) * ROWS, ROWS), :] for t in range(groups - 1)
-        )
-        split = jnp.where(
-            lane < LANES - rest,
-            pltpu.roll(first, LANES - rest, 1),
-            pltpu.roll(second, 2 * LANES - 2 * rest, 1),
-        )
-        return [jnp.concatenate(x + [tail], axis=1) for x, tail in zip(found, (first, second, third, split))]
+            send[way, level, edge_slot(0, 2, 0), :] = first
+            send[way, level, edge_slot(0, 2, 1), :] = second
+            send[way, level, edge_slot(1, 2, 0), :] = third
+
+    def edges_of(way, level, quad):
+        found = [[recv[way, level, edge_slot(quad, field, t), :] for t in range(full)] for field in range(2)]
+        first, second = (recv[way, level, edge_slot(0, 2, t), :] for t in range(2))
+        if quad:
+            third = recv[way, level, edge_slot(1, 2, 0), :]
+            split = jnp.where(
+                lane < LANES - rest,
+                pltpu.roll(first, LANES - rest, 1),
+                pltpu.roll(second, 2 * LANES - 2 * rest, 1),
+            )
+            first, second = third, split
+        return [jnp.concatenate(x + [tail], axis=1) for x, tail in zip(found, (first, second))]
+
+    def all_edges(level):
+        return [edge_copy(way, level, quad) for quad in range(quads) for way in range(2)]
 
     wind_copy(0).wait()
     pack(0)
@@ -141,8 +147,8 @@
     def _(level):
         wind_copy(level).wait()
         pack(level)
-        edge_copy(0, level - 1).start()
-        edge_copy(1, level - 1).start()
+        for copy in all_edges(level - 1):
+            copy.start()
         old_copy(level - 1).start()
 
     old_copy(levels - 1).start()
@@ -151,8 +157,8 @@
         copy.wait()
     keep[...] = padded(ground[...], width)
     total[...] = jnp.zeros_like(total)
-    edge_copy(0, levels - 1).start()
-    edge_copy(1, levels - 1).start()
+    for copy in all_edges(levels - 1):
+        copy.start()
 
     @pl.loop(0, levels)
     def _(level):
@@ -184,17 +190,18 @@
         total[...] += out
 
     def snapshots(level):
-        edge_copy(0, level).wait_recv()
-        edge_copy(1, level).wait_recv()
         cos = cosine[...]
         scale = jnp.where(band * levels + level < keep[...], factor[...], 0.0)
-        arrived = [edges_of(way, level) for way in range(2)]
         for pair in range(snaps // 2):
+            if pair % 2 == 0:
+                for way in range(2):
+                    edge_copy(way, level, pair // 2).wait_recv()
+                arrived = [edges_of(way, level, pair // 2) for way in range(2)]
             found = [[], []]
             for snap in (2 * pair, 2 * pair + 1):
                 quad, j = divmod(snap, 4)
                 east, north = (padded(wind[field, snap, level], width) for field in range(2))
-                edges = [[arrived[way][field * quads + quad] for way in (1, 0)] for field in range(2)]
+                edges = [[arrived[way][field] for way in (1, 0)] for field in range(2)]
                 found[0].append((along_lon(north, edges[1], j) - along_lat(east * cos)) * scale)
                 found[1].append((along_lon(east, edges[0], j) + along_lat(north * cos)) * scale)
             for field in range(2):
@@ -264,8 +271,8 @@
 
     @pl.loop(0, levels)
     def _(level):
-        edge_copy(0, level).wait_send()
-        edge_copy(1, level).wait_send()
+        for copy in all_edges(level):
+            copy.wait_send()
 
 
 def over_rows(x):
@@ -302,8 +309,10 @@
     levels, fields, _, lat = new_basis.shape[1:]
     size = side // ROWS
 
-    def out_copy(level, slot):
-        return pltpu.make_async_copy(out.at[slot], new_basis.at[:, level], out_sem.at[slot])
+    def out_copy(level, slot, field):
+        return pltpu.make_async_copy(
+            out.at[slot, :, field], new_basis.at[:, level, field], out_sem.at[slot, field]
+        )
 
     packed = gram[...]
     block = jnp.concatenate([turned(packed, -q * size, 1) for q in range(size // ROWS)], axis=0)
@@ -346,17 +355,19 @@
 
         @pl.when(level >= slots)
         def _():
-            out_copy(level - slots, slot).wait()
+            for field in range(fields):
+                out_copy(level - slots, slot, field).wait()
 
         for field in range(fields):
             found = jnp.dot(weights[...], cols[fields * level + field], preferred_element_type=jnp.float32)
             found = found[: rank * ROWS] + found[rank * ROWS :]
             out[slot, :, field] = found[:, :lat].reshape(rank, ROWS, lat)
-        out_copy(level, slot).start()
+            out_copy(level, slot, field).start()
 
     @pl.loop(levels - slots, levels)
     def _(level):
-        out_copy(level, lax.rem(level, slots)).wait()
+        for field in range(fields):
+            out_copy(level, lax.rem(level, slots), field).wait()
 
 
 def in_hbm(x):
@@ -407,8 +418,8 @@
             pltpu.SemaphoreType.DMA((3,)),
             pltpu.SemaphoreType.DMA((levels,)),
             pltpu.SemaphoreType.DMA((levels,)),
-            pltpu.SemaphoreType.DMA((2, levels)),
-            pltpu.SemaphoreType.DMA((2, levels)),
+            pltpu.SemaphoreType.DMA((2, levels, 2)),
+            pltpu.SemaphoreType.DMA((2, levels, 2)),
             pltpu.SemaphoreType.DMA((near_n,)),
             pltpu.SemaphoreType.DMA((near_n,)),
             pltpu.SemaphoreType.DMA((far_n,)),
@@ -428,7 +439,7 @@
             pltpu.VMEM((2 * rank * ROWS, side), jnp.bfloat16),
             pltpu.VMEM((size, size, LANES), jnp.float32),
             pltpu.VMEM((SLOTS, rank, 2, ROWS, lat), jnp.float32),
-            pltpu.SemaphoreType.DMA((SLOTS,)),
+            pltpu.SemaphoreType.DMA((SLOTS, 2)),
         ],
         compiler_params=pltpu.CompilerParams(vmem_limit_bytes=PROJECT_VMEM),
         name="project",

time: 45.8 us -> 46 us (level)
  no operation moved by 1% of the time
where the time goes in v3:
time: 46 us; the launch traced here: 45.9 us
  Pallas kernels  45.8 us (100%)
    pallas_call x1, Pallas kernels, on_device(): pl.pallas_call(functools.partial(gather_kernel, bands, tiles, rank, snaps...  35 us
    pallas_call x1, Pallas kernels, on_device(): pl.pallas_call(functools.partial(project_kernel, rank), out_shape=jax.Sha...  10.8 us

profile of v3, /device:TPU:0, one launch (start us, length us, event | category | flops | bytes accessed | tf_op | source)
XLA Modules:
  0.0 45.9 jit_solution(13193828187858557284)
XLA Ops:
  0.0 35.0 %gather.1 = (bf16[24,256,768]{2,1,0:T(8,128)(2,1)S(1)}, f32[8,128]{1,0:T(8,128)S(1)}) custom-call(f32[2,8,12,8,720]{4,3,2,1,0:T(8,128)} %winds.1, bf16[24,12,2,8,720]{4,3,2,1,0:T(8,128)(2,1)} %basis.1, s32[8,720]{1,0:T(8,128)} %ground_in.1, f32[8,768]{1,0:T(8,128)} %constant.4.clone.cosine_in, f32[8,768]{1,0:T(8,128)} %constant.5.clone.factor_in), custom_call_target="tpu_custom_call" | custom-call | tf_op jit(solution)/shard_map/gather/pallas_call | solution.py:397
  35.0 10.8 %project.1 = f32[24,12,2,8,720]{4,3,2,1,0:T(8,128)} custom-call(f32[8,128]{1,0:T(8,128)S(1)} %get-tuple-element.7.gram, bf16[24,256,768]{2,1,0:T(8,128)(2,1)S(1)} %get-tuple-element.8.cols), custom_call_target="tpu_custom_call" | custom-call | tf_op jit(solution)/shard_map/project/pallas_call | solution.py:433

commit v4 on v2

--- a/solution.py
+++ b/solution.py
@@ -39,13 +39,13 @@
     bands, tiles, rank, snaps,
     winds, basis, ground_in, cosine_in, factor_in,
     cols, gram,
-    wind, old, send, recv, ground, cosine, factor, keep, total, near, far, across,
-    small_sem, wind_sem, old_sem, send_sem, recv_sem, near_send, near_recv, far_send, far_recv, across_send, across_recv,
+    wind, old, send, recv, ground, cosine, factor, keep, total, near, far,
+    small_sem, wind_sem, old_sem, send_sem, recv_sem, near_send, near_recv, far_send, far_recv,
 ):
     levels = winds.shape[2]
     lat = winds.shape[4]
     width = cols.shape[2]
-    near_n, far_n = near.shape[0], far.shape[0]
+    near_n = near.shape[0]
     quads = snaps // 4
     band = lax.axis_index("band")
     tile = lax.axis_index("tile")
@@ -71,11 +71,22 @@
     wind_copy(0).start()
     near_at = lax.rem(tile, near_n)
     far_at = lax.div(tile, near_n)
-    near_peers = [(band, far_at * near_n + lax.rem(near_at + d, near_n)) for d in range(1, near_n)]
-    far_peers = [(band, lax.rem(tile + d * near_n, tiles)) for d in range(1, far_n)]
-    band_peers = [(lax.rem(band + d, bands), tile) for d in range(1, bands)]
+    near_peers = [
+        (lax.rem(near_at + d, near_n), (band, far_at * near_n + lax.rem(near_at + d, near_n)))
+        for d in sorted(range(1, near_n), key=lambda d: abs(d - near_n // 2))
+    ]
+    wide_n = tiles // near_n
+    apart = [(dy, dx) for dy in range(bands) for dx in range(wide_n) if dy or dx]
+    apart.sort(key=lambda at: -(min(at[0], bands - at[0]) + min(at[1], wide_n - at[1])))
+    far_peers = [
+        (
+            lax.rem(band + dy, bands) * wide_n + lax.rem(far_at + dx, wide_n),
+            (lax.rem(band + dy, bands), lax.rem(tile + dx * near_n, tiles)),
+        )
+        for dy, dx in apart
+    ]
     barrier = pltpu.get_barrier_semaphore()
-    greeted = [(band, left), (band, right)] + near_peers + far_peers + band_peers
+    greeted = [(band, left), (band, right)] + [peer for _, peer in near_peers + far_peers]
     for peer in greeted:
         pl.semaphore_signal(barrier, inc=1, device_id=peer, device_id_type=MESH)
 
@@ -245,21 +256,19 @@
                 device_id_type=MESH,
             )
 
-        n = box.shape[0]
-        for d, peer in enumerate(peers):
+        for d, (_, peer) in enumerate(peers):
             copy(at, d, peer).start()
-        for d, peer in enumerate(peers):
-            copy(lax.rem(at + d + 1, n), d, peer).wait_recv()
+        for d, (slot, peer) in enumerate(peers):
+            copy(slot, d, peer).wait_recv()
         out = box[0]
-        for slot in range(1, n):
+        for slot in range(1, box.shape[0]):
             out = out + box[slot]
-        for d, peer in enumerate(peers):
+        for d, (_, peer) in enumerate(peers):
             copy(at, d, peer).wait_send()
         return out
 
     part = summed(part, near, near_at, near_peers, near_recv, near_send)
-    part = summed(part, far, far_at, far_peers, far_recv, far_send)
-    part = summed(part, across, band, band_peers, across_recv, across_send)
+    part = summed(part, far, band * wide_n + far_at, far_peers, far_recv, far_send)
     gram[...] = part
 
     @pl.loop(0, levels)
@@ -378,7 +387,8 @@
     size = rank + snaps
     side = size * ROWS
     width = -(-lat // LANES) * LANES
-    near_n, far_n = 8, tiles // 8
+    near_n = 8
+    far_n = bands * (tiles // near_n)
     cosine, factor = constants(lat, width)
     whole = pl.BlockSpec(memory_space=pltpu.VMEM)
     anywhere = pl.BlockSpec(memory_space=pltpu.HBM)
@@ -403,7 +413,6 @@
             pltpu.VMEM((side, side), jnp.float32),
             pltpu.VMEM((near_n, ROWS, LANES), jnp.float32),
             pltpu.VMEM((far_n, ROWS, LANES), jnp.float32),
-            pltpu.VMEM((bands, ROWS, LANES), jnp.float32),
             pltpu.SemaphoreType.DMA((3,)),
             pltpu.SemaphoreType.DMA((levels,)),
             pltpu.SemaphoreType.DMA((levels,)),
@@ -413,8 +422,6 @@
             pltpu.SemaphoreType.DMA((near_n,)),
             pltpu.SemaphoreType.DMA((far_n,)),
             pltpu.SemaphoreType.DMA((far_n,)),
-            pltpu.SemaphoreType.DMA((bands,)),
-            pltpu.SemaphoreType.DMA((bands,)),
         ],
         compiler_params=pltpu.CompilerParams(collective_id=0, has_side_effects=True, vmem_limit_bytes=GATHER_VMEM),
         name="gather",

time: 45.8 us -> 43.9 us (0.959)
  Pallas kernels: 45.7 us -> 43.7 us
    pallas_call x1, Pallas kernels: 34.8 us -> 32.8 us  [on_device(): pl.pallas_call(functools.partial(gather_kernel, bands, tiles, rank, snaps...]
where the time goes in v4:
time: 43.9 us; the launch traced here: 43.7 us
  Pallas kernels  43.7 us (100%)
    pallas_call x1, Pallas kernels, on_device(): pl.pallas_call(functools.partial(gather_kernel, bands, tiles, rank, snaps...  32.8 us
    pallas_call x1, Pallas kernels, on_device(): pl.pallas_call(functools.partial(project_kernel, rank), out_shape=jax.Sha...  10.9 us

profile of v4, /device:TPU:0, one launch (start us, length us, event | category | flops | bytes accessed | tf_op | source)
XLA Modules:
  0.0 43.7 jit_solution(1657438752317790974)
XLA Ops:
  0.0 32.8 %gather.1 = (bf16[24,256,768]{2,1,0:T(8,128)(2,1)S(1)}, f32[8,128]{1,0:T(8,128)S(1)}) custom-call(f32[2,8,12,8,720]{4,3,2,1,0:T(8,128)} %winds.1, bf16[24,12,2,8,720]{4,3,2,1,0:T(8,128)(2,1)} %basis.1, s32[8,720]{1,0:T(8,128)} %ground_in.1, f32[8,768]{1,0:T(8,128)} %constant.4.clone.cosine_in, f32[8,768]{1,0:T(8,128)} %constant.5.clone.factor_in), custom_call_target="tpu_custom_call" | custom-call | tf_op jit(solution)/shard_map/gather/pallas_call | solution.py:396
  32.8 10.9 %project.1 = f32[24,12,2,8,720]{4,3,2,1,0:T(8,128)} custom-call(f32[8,128]{1,0:T(8,128)S(1)} %get-tuple-element.7.gram, bf16[24,256,768]{2,1,0:T(8,128)(2,1)S(1)} %get-tuple-element.8.cols), custom_call_target="tpu_custom_call" | custom-call | tf_op jit(solution)/shard_map/project/pallas_call | solution.py:429
